TPU v7x, 32 devices: a whole 2x2x4 slice. The times are simulated.
32 devices in a mesh: dp: 8 (over z, x), tensor: 4 (over y, core).
Axes of the slice: x: 2, y: 2, z: 4, core: 2. Of those that a mesh axis runs over, the one named last changes fastest.
Arguments:
- inputs: bfloat16 [8192, 2048], P('dp'), may hold values from -6 to 6
- first_gain: float32 [2048], replicated, may hold values from 0.25 to 1.75
- first_bias: float32 [2048], replicated, may hold values from -1.75 to 1.75
- query_weight: bfloat16 [2048, 2048], P(None, 'tensor'), may hold values from -0.125 to 0.125
- query_bias: float32 [2048], P('tensor'), may hold values from -1.75 to 1.75
- keyval_weight: bfloat16 [2048, 256], replicated, may hold values from -0.1875 to 0.1875
- value_bias: float32 [128], replicated, may hold values from -3 to 3
- output_weight: bfloat16 [2048, 2048], P('tensor'), may hold values from -1 to 1
- output_bias: float32 [2048], replicated, may hold values from -1.75 to 1.75
- second_gain: float32 [2048], replicated, may hold values from 0.25 to 1.75
- second_bias: float32 [2048], replicated, may hold values from -1.75 to 1.75
- up_weight: bfloat16 [2048, 8192], P(None, 'tensor'), may hold values from -0.125 to 0.125
- up_bias: float32 [8192], P('tensor'), may hold values from -1.75 to 1.75
- down_weight: bfloat16 [8192, 2048], P('tensor'), may hold values from -0.09375 to 0.09375
- down_bias: float32 [2048], replicated, may hold values from -1.75 to 1.75
- cotangent: bfloat16 [8192, 2048], P('dp'), may hold values from -6 to 6
Outputs:
- layer_out: bfloat16 [8192, 2048], P('dp')
- grad_inputs: float32 [8192, 2048], P('dp')
- grad_first_gain: float32 [2048], replicated
- grad_first_bias: float32 [2048], replicated
- grad_query_weight: float32 [2048, 2048], P('dp', 'tensor')
- grad_query_bias: float32 [2048], P('tensor')
- grad_keyval_weight: float32 [2048, 256], P('dp')
- grad_value_bias: float32 [128], replicated
- grad_output_weight: float32 [2048, 2048], P('tensor', 'dp')
- grad_output_bias: float32 [2048], replicated
- grad_second_gain: float32 [2048], replicated
- grad_second_bias: float32 [2048], replicated
- grad_up_weight: float32 [2048, 8192], P('dp', 'tensor')
- grad_up_bias: float32 [8192], P('tensor')
- grad_down_weight: float32 [8192, 2048], P('tensor', 'dp')
- grad_down_bias: float32 [2048], replicated
All inputs are finite; a program needn't handle non-finite values.
Results may differ from a plain program's by a relative error of at most 0.024.
Values may be sent and summed in bfloat16 or wider, within the bound.
A program may use at most 320 MiB of HBM per device.

v0:
```python
from functools import partial
import jax
import jax.numpy as jnp
from jax import lax
from jax.sharding import PartitionSpec as P

SPAN = 8
EPSILON = 1e-05
NEG_LARGE = -1e30


def shifted(value, axis, steps):
    count = lax.axis_size(axis)
    first, last = (max(0, -steps), min(count, count - steps))
    return lax.ppermute(value, axis, [(source, source + steps) for source in range(first, last)])


def layer_norm(values, norm_gain, norm_bias):
    average = jnp.mean(values, axis=-1, keepdims=True)
    centred = values - average
    variance = jnp.mean(centred * centred, axis=-1, keepdims=True)
    return centred * lax.rsqrt(variance + EPSILON) * norm_gain + norm_bias


def gelu_tanh(values):
    return jax.nn.gelu(values, approximate=True)


def over_rows(left, right):
    return lax.dot_general(
        left, right, (((0,), (0,)), ((), ())), preferred_element_type=jnp.float32
    )


def over_cols(left, right):
    return lax.dot_general(
        left, right, (((1,), (1,)), ((), ())), preferred_element_type=jnp.float32
    )


def per_device(
    inputs,
    first_gain,
    first_bias,
    query_weight,
    query_bias,
    keyval_weight,
    value_bias,
    output_weight,
    output_bias,
    second_gain,
    second_bias,
    up_weight,
    up_bias,
    down_weight,
    down_bias,
    cotangent,
):
    tok_rows = inputs.shape[0]
    head_size = value_bias.shape[0]
    local_heads = query_weight.shape[1] // head_size
    score_scale = head_size ** (-0.5)
    position = lax.axis_index("dp") % SPAN
    causal = jnp.arange(tok_rows)[:, None] >= jnp.arange(tok_rows)[None, :]
    x_full = inputs.astype(jnp.float32)
    normed1_full, first_pull = jax.vjp(layer_norm, x_full, first_gain, first_bias)
    normed1 = normed1_full.astype(jnp.bfloat16)
    query_pre = jnp.dot(normed1, query_weight, preferred_element_type=jnp.float32) + query_bias
    queries = (
        (query_pre * score_scale).astype(jnp.bfloat16).reshape(tok_rows, local_heads, head_size)
    )
    kv_bias = jnp.concatenate([jnp.zeros_like(value_bias), value_bias])
    keyval = (jnp.dot(normed1, keyval_weight, preferred_element_type=jnp.float32) + kv_bias).astype(
        jnp.bfloat16
    )

    def score_block(kv_block, diagonal):
        scores = jnp.einsum(
            "qhd,kd->hqk", queries, kv_block[:, :head_size], preferred_element_type=jnp.float32
        )
        if diagonal:
            scores = jnp.where(causal[None], scores, NEG_LARGE)
        return scores

    def fold_stats(carried, kv_block, diagonal):
        run_peak, run_total = carried
        scores = score_block(kv_block, diagonal)
        new_peak = jnp.maximum(run_peak, jnp.max(scores, axis=-1))
        run_total = run_total * jnp.exp(run_peak - new_peak) + jnp.sum(
            jnp.exp(scores - new_peak[..., None]), axis=-1
        )
        return (new_peak, run_total)

    def keep_first(carried, kv_block):
        return carried

    kv_blocks = [keyval]
    for offset in range(1, SPAN):
        kv_blocks.append(shifted(keyval, "dp", offset))
    running = (
        jnp.full((local_heads, tok_rows), NEG_LARGE, jnp.float32),
        jnp.zeros((local_heads, tok_rows), jnp.float32),
    )
    for offset in range(SPAN):
        if offset == 0:
            running = fold_stats(running, kv_blocks[0], True)
        else:
            running = lax.cond(
                offset <= position,
                partial(fold_stats, diagonal=False),
                keep_first,
                running,
                kv_blocks[offset],
            )
    log_total = running[0] + jnp.log(running[1])

    def fold_context(carried, kv_block, diagonal):
        attn_probs = jnp.exp(score_block(kv_block, diagonal) - log_total[..., None]).astype(
            jnp.bfloat16
        )
        return carried + jnp.einsum(
            "hqk,kd->qhd", attn_probs, kv_block[:, head_size:], preferred_element_type=jnp.float32
        )

    context = jnp.zeros((tok_rows, local_heads, head_size), jnp.float32)
    for offset in range(SPAN):
        if offset == 0:
            context = fold_context(context, kv_blocks[0], True)
        else:
            context = lax.cond(
                offset <= position,
                partial(fold_context, diagonal=False),
                keep_first,
                context,
                kv_blocks[offset],
            )
    context_low = context.reshape(tok_rows, -1).astype(jnp.bfloat16)
    attn_part = jnp.dot(context_low, output_weight, preferred_element_type=jnp.float32)
    middle = (
        x_full
        + lax.psum(attn_part.astype(jnp.bfloat16), "tensor").astype(jnp.float32)
        + output_bias
    )
    normed2_full, second_pull = jax.vjp(layer_norm, middle, second_gain, second_bias)
    normed2 = normed2_full.astype(jnp.bfloat16)
    pre_act = jnp.dot(normed2, up_weight, preferred_element_type=jnp.float32) + up_bias
    act_full, gelu_pull = jax.vjp(gelu_tanh, pre_act)
    activ = act_full.astype(jnp.bfloat16)
    mlp_part = jnp.dot(activ, down_weight, preferred_element_type=jnp.float32)
    result = (
        middle + lax.psum(mlp_part.astype(jnp.bfloat16), "tensor").astype(jnp.float32) + down_bias
    )
    layer_out = result.astype(jnp.bfloat16)
    grad_full = cotangent.astype(jnp.float32)
    d_down_bias = jnp.sum(grad_full, axis=0)
    grad_down_part = over_rows(activ, cotangent)
    d_pre = gelu_pull(over_cols(cotangent, down_weight))[0].astype(jnp.bfloat16)
    grad_up_part = over_rows(normed2, d_pre)
    d_up_bias = jnp.sum(d_pre.astype(jnp.float32), axis=0)
    d_normed2 = lax.psum(over_cols(d_pre, up_weight).astype(jnp.bfloat16), "tensor").astype(
        jnp.float32
    )
    d_middle_norm, d_second_gain, d_second_bias = second_pull(d_normed2)
    d_middle = grad_full + d_middle_norm
    d_output_bias = jnp.sum(d_middle, axis=0)
    d_middle_low = d_middle.astype(jnp.bfloat16)
    grad_out_part = over_rows(context_low, d_middle_low)
    d_context = (
        over_cols(d_middle_low, output_weight)
        .astype(jnp.bfloat16)
        .reshape(tok_rows, local_heads, head_size)
    )
    delta = jnp.einsum("qhd,qhd->hq", d_context.astype(jnp.float32), context)

    def block_grads(kv_block, diagonal):
        key_rows = kv_block[:, :head_size]
        value_rows = kv_block[:, head_size:]
        attn_probs = jnp.exp(score_block(kv_block, diagonal) - log_total[..., None])
        d_probs = jnp.einsum(
            "qhd,kd->hqk", d_context, value_rows, preferred_element_type=jnp.float32
        )
        d_scores = (attn_probs * (d_probs - delta[..., None])).astype(jnp.bfloat16)
        d_query = jnp.einsum("hqk,kd->qhd", d_scores, key_rows, preferred_element_type=jnp.float32)
        d_key = jnp.einsum("hqk,qhd->kd", d_scores, queries, preferred_element_type=jnp.float32)
        d_value = jnp.einsum(
            "hqk,qhd->kd",
            attn_probs.astype(jnp.bfloat16),
            d_context,
            preferred_element_type=jnp.float32,
        )
        return (d_query, jnp.concatenate([d_key, d_value], axis=1))

    def no_grads(kv_block):
        return (
            jnp.zeros((tok_rows, local_heads, head_size), jnp.float32),
            jnp.zeros((tok_rows, 2 * head_size), jnp.float32),
        )

    d_query_sum = jnp.zeros((tok_rows, local_heads, head_size), jnp.float32)
    d_kv_sum = jnp.zeros((tok_rows, 2 * head_size), jnp.float32)
    for offset in range(SPAN):
        if offset == 0:
            kv_block = keyval
        else:
            kv_block = shifted(keyval, "dp", offset)
        if offset == 0:
            d_query_part, d_kv_part = block_grads(kv_block, True)
            d_kv_sum = d_kv_part
        else:
            d_query_part, d_kv_part = lax.cond(
                offset <= position, partial(block_grads, diagonal=False), no_grads, kv_block
            )
            d_kv_sum = d_kv_sum + shifted(d_kv_part.astype(jnp.bfloat16), "dp", -offset).astype(
                d_kv_part.dtype
            )
        d_query_sum = d_query_sum + d_query_part
    d_queries = (d_query_sum * score_scale).reshape(tok_rows, -1).astype(jnp.bfloat16)
    grad_query_part = over_rows(normed1, d_queries)
    d_query_bias = jnp.sum(d_queries.astype(jnp.float32), axis=0)
    d_normed1_query = over_cols(d_queries, query_weight)
    d_normed1_sum, d_kv_total = (
        lax.psum(d_normed1_query.astype(jnp.bfloat16), "tensor").astype(jnp.float32),
        lax.psum(d_kv_sum.astype(jnp.bfloat16), "tensor").astype(jnp.float32),
    )
    d_keyval = d_kv_total.astype(jnp.bfloat16)
    grad_kv_part = over_rows(normed1, d_keyval)
    d_value_bias = jnp.sum(d_keyval[:, head_size:].astype(jnp.float32), axis=0)
    d_normed1 = d_normed1_sum + over_cols(d_keyval, keyval_weight)
    d_x_norm, d_first_gain, d_first_bias = first_pull(d_normed1)
    grad_inputs = d_middle + d_x_norm
    sent_query, sent_kv, sent_out, sent_up, sent_down = (
        lax.psum_scatter(
            grad_query_part.astype(jnp.bfloat16), "dp", scatter_dimension=0, tiled=True
        ).astype(jnp.float32),
        lax.psum_scatter(
            grad_kv_part.astype(jnp.bfloat16), "dp", scatter_dimension=0, tiled=True
        ).astype(jnp.float32),
        lax.psum_scatter(
            grad_out_part.astype(jnp.bfloat16), "dp", scatter_dimension=1, tiled=True
        ).astype(jnp.float32),
        lax.psum_scatter(
            grad_up_part.astype(jnp.bfloat16), "dp", scatter_dimension=0, tiled=True
        ).astype(jnp.float32),
        lax.psum_scatter(
            grad_down_part.astype(jnp.bfloat16), "dp", scatter_dimension=1, tiled=True
        ).astype(jnp.float32),
    )
    bias_sums = (
        lax.psum(d_first_gain.astype(jnp.bfloat16), "dp").astype(jnp.float32),
        lax.psum(d_first_bias.astype(jnp.bfloat16), "dp").astype(jnp.float32),
        lax.psum(d_query_bias.astype(jnp.bfloat16), "dp").astype(jnp.float32),
        lax.psum(d_value_bias.astype(jnp.bfloat16), "dp").astype(jnp.float32),
        lax.psum(d_output_bias.astype(jnp.bfloat16), "dp").astype(jnp.float32),
        lax.psum(d_second_gain.astype(jnp.bfloat16), "dp").astype(jnp.float32),
        lax.psum(d_second_bias.astype(jnp.bfloat16), "dp").astype(jnp.float32),
        lax.psum(d_up_bias.astype(jnp.bfloat16), "dp").astype(jnp.float32),
        lax.psum(d_down_bias.astype(jnp.bfloat16), "dp").astype(jnp.float32),
    )
    return (
        layer_out,
        grad_inputs,
        bias_sums[0],
        bias_sums[1],
        sent_query,
        bias_sums[2],
        sent_kv,
        bias_sums[3],
        sent_out,
        bias_sums[4],
        bias_sums[5],
        bias_sums[6],
        sent_up,
        bias_sums[7],
        sent_down,
        bias_sums[8],
    )


def solution(mesh):
    in_specs = (
        P("dp", None),
        P(),
        P(),
        P(None, "tensor"),
        P("tensor"),
        P(),
        P(),
        P("tensor", None),
        P(),
        P(),
        P(),
        P(None, "tensor"),
        P("tensor"),
        P("tensor", None),
        P(),
        P("dp", None),
    )
    out_specs = (
        P("dp", None),
        P("dp", None),
        P(),
        P(),
        P("dp", "tensor"),
        P("tensor"),
        P("dp", None),
        P(),
        P("tensor", "dp"),
        P(),
        P(),
        P(),
        P("dp", "tensor"),
        P("tensor"),
        P("tensor", "dp"),
        P(),
    )
    return jax.shard_map(
        per_device, mesh=mesh, in_specs=in_specs, out_specs=out_specs, check_vma=False
    )
```

profile of v0, /device:TPU:0, one launch (start us, length us, event | category | flops | bytes accessed | tf_op | source)
XLA Modules:
  0.0 1510.2 jit_solution(6930662168636804116)
XLA Ops:
  46.4 24.7 %collective-permute-done.1 = bf16[1024,256]{1,0:T(8,128)(2,1)} collective-permute-done((bf16[1024,256]{1,0:T(8,128)(2,1)}, bf16[1024,256]{1,0:T(8,128)(2,1)}, u32[]{:S(2)}, u32[]{:S(2)}) %collective-permute-start.1) | collective-permute-done | bytes 524320 | tf_op jit(solution)/shard_map/ppermute | solution.py:15
  71.2 17.3 %collective-permute-start.3 = (bf16[1024,256]{1,0:T(8,128)(2,1)}, bf16[1024,256]{1,0:T(8,128)(2,1)}, u32[]{:S(2)}, u32[]{:S(2)}) collective-permute-start(bf16[1024,256]{1,0:T(8,128)(2,1)} %fusion.260), channel_id=1, source_target_pairs={{0,16},{4,20},{8,24},{12,28},{1,17},{5,21},{9,25},{13,29},{2,18},{... | collective-permute-start | bytes 1572872 | tf_op jit(solution)/shard_map/ppermute | solution.py:15
  124.6 11.6 convolution_bitcast_fusion.14
  164.9 194.8 %all-reduce.7.cloned.1.call-done = bf16[1024,2048]{1,0:T(8,128)(2,1)} async-done(((bf16[1024,2048]{1,0:T(8,128)(2,1)}), bf16[1024,2048]{1,0:T(8,128)(2,1)}) %all-reduce.7.cloned.1.call-update) | async-done | bytes 4194320 | tf_op jit(solution)/shard_map/psum | solution.py:141
  368.6 13.9 fusion.277
  382.5 20.6 %fusion.282 = (bf16[2048]{0:T(1024)(128)(2,1)}, bf16[1024,2048]{1,0:T(8,128)(2,1)}) fusion(f32[1024,2048]{1,0:T(8,128)} %fusion.277, f32[2048]{0:T(1024)S(1)} %copy-done.60, bf16[1024,2048]{1,0:T(8,128)(2,1)S(1)} %copy-done.22, bf16[2048,2048]{1,0:T(8,128)(2,1)} %param.71), kind=kOutput, calls=%fused_computation.363 | convolution fusion | flops 8636069888 | bytes 25178112 | tf_op jit(solution)/shard_map/dot_general | solution.py:36
  403.1 12.2 convolution_convert_fusion.3
  415.3 16.0 %convolution_convert_fusion.4 = bf16[1024,2048]{1,0:T(8,128)(2,1)} fusion(bf16[2048,2048]{1,0:T(8,128)(2,1)} %param.71, f32[1024,2048]{1,0:T(8,128)} %fusion.277, f32[2048]{0:T(1024)S(1)} %copy-done.60), kind=kOutput, calls=%fused_computation.306 | convolution fusion | flops 8613003264 | bytes 20979712 | tf_op jit(solution)/shard_map/dot_general | solution.py:149
  431.4 69.7 %all-reduce.9.cloned.1.call-done = bf16[1024,2048]{1,0:T(8,128)(2,1)} async-done(((bf16[1024,2048]{1,0:T(8,128)(2,1)}), bf16[1024,2048]{1,0:T(8,128)(2,1)}) %all-reduce.9.cloned.1.call-update) | async-done | bytes 4194320 | tf_op jit(solution)/shard_map/psum | solution.py:160
  606.6 30.9 %collective-permute-done.8 = bf16[1024,256]{0,1:T(8,128)(2,1)} collective-permute-done((bf16[1024,256]{0,1:T(8,128)(2,1)}, bf16[1024,256]{0,1:T(8,128)(2,1)}, u32[]{:S(2)}, u32[]{:S(2)}) %collective-permute-start.8) | collective-permute-done | bytes 524320 | tf_op jit(solution)/shard_map/ppermute | solution.py:15
  649.6 21.3 %collective-permute-done.9 = bf16[1024,256]{0,1:T(8,128)(2,1)} collective-permute-done((bf16[1024,256]{0,1:T(8,128)(2,1)}, bf16[1024,256]{0,1:T(8,128)(2,1)}, u32[]{:S(2)}, u32[]{:S(2)}) %collective-permute-start.9) | collective-permute-done | bytes 524320 | tf_op jit(solution)/shard_map/ppermute | solution.py:15
  670.9 45.3 %collective-permute-done.10 = bf16[1024,256]{0,1:T(8,128)(2,1)} collective-permute-done((bf16[1024,256]{0,1:T(8,128)(2,1)}, bf16[1024,256]{0,1:T(8,128)(2,1)}, u32[]{:S(2)}, u32[]{:S(2)}) %collective-permute-start.10) | collective-permute-done | bytes 524320 | tf_op jit(solution)/shard_map/ppermute | solution.py:15
  716.3 33.6 %collective-permute-done.11 = bf16[1024,256]{0,1:T(8,128)(2,1)} collective-permute-done((bf16[1024,256]{0,1:T(8,128)(2,1)}, bf16[1024,256]{0,1:T(8,128)(2,1)}, u32[]{:S(2)}, u32[]{:S(2)}) %collective-permute-start.11) | collective-permute-done | bytes 524320 | tf_op jit(solution)/shard_map/ppermute | solution.py:15
  749.9 31.8 %collective-permute-done.12 = bf16[1024,256]{0,1:T(8,128)(2,1)S(1)} collective-permute-done((bf16[1024,256]{0,1:T(8,128)(2,1)S(1)}, bf16[1024,256]{0,1:T(8,128)(2,1)S(1)}, u32[]{:S(2)}, u32[]{:S(2)}) %collective-permute-start.12) | collective-permute-done | bytes 524320 | tf_op jit(solution)/shard_map/ppermute | solution.py:15
  781.6 43.0 %collective-permute-done.13 = bf16[1024,256]{0,1:T(8,128)(2,1)S(1)} collective-permute-done((bf16[1024,256]{0,1:T(8,128)(2,1)S(1)}, bf16[1024,256]{0,1:T(8,128)(2,1)S(1)}, u32[]{:S(2)}, u32[]{:S(2)}) %collective-permute-start.13) | collective-permute-done | bytes 524320 | tf_op jit(solution)/shard_map/ppermute | solution.py:15
  842.1 144.8 %all-reduce.11.cloned.1.call-done = (bf16[1024,2048]{1,0:T(8,128)(2,1)}, bf16[1024,2048]{1,0:T(8,128)(2,1)}, bf16[1024,256]{0,1:T(8,128)(2,1)}) async-done(((bf16[1024,2048]{1,0:T(8,128)(2,1)}, bf16[1024,2048]{1,0:T(8,128)(2,1)}, bf16[1024,256]{0,1:T(8,128)(2,1)}), (bf16[1024,2048]{1,0:T(8,128)(2,1)}, bf16[1024,2048]{1,0:T(8,128)(2,1)}, bf16[1024,256]{0,1:T(8,128)(2,1)})) %all-reduce.11.cloned.1.call-update) | async-done | bytes 8912912 | tf_op jit(solution)/shard_map/psum | solution.py:151
  991.9 15.9 %convolution_convert_fusion = bf16[2048,2048]{1,0:T(8,128)(2,1)} fusion(bf16[1024,2048]{1,0:T(8,128)(2,1)} %param.73, f32[1024,2048]{1,0:T(8,128)} %fusion.277, f32[2048]{0:T(1024)S(1)} %copy-done.61), kind=kOutput, calls=%fused_computation.299 | convolution fusion | flops 8615100416 | bytes 20979712 | tf_op jit(solution)/shard_map/dot_general | solution.py:30
  1008.6 15.5 %convolution_convert_fusion.1 = bf16[2048,2048]{1,0:T(8,128)(2,1)} fusion(bf16[1024,2048]{1,0:T(8,128)(2,1)} %get-tuple-element.562, f32[2048]{0:T(1024)S(1)} %copy-done.63, f32[2048]{0:T(1024)S(1)} %copy-done.43, f32[1024]{0:T(1024)S(1)} %copy-done.49, bf16[1024,2048]{1,0:T(8,128)(2,1)} %all-reduce.7.cloned.1.call-done, bf16[1024,2048]{1,0:T(8,128)(2,1)} %param.58, ...), kind=kOutput, calls=%fused_computation.300 | convolution fusion | flops 8613003264 | bytes 21004288 | tf_op jit(solution)/shard_map/dot_general | solution.py:30
  1029.9 29.5 %reduce-scatter.10.cloned.1.call-done = bf16[512,256]{1,0:T(8,128)(2,1)} async-done(((bf16[512,2048]{1,0:T(8,128)(2,1)}), bf16[512,256]{1,0:T(8,128)(2,1)}) %reduce-scatter.10.cloned.1.call-update) | async-done | bytes 262160 | tf_op jit(solution)/shard_map/reduce_scatter | solution.py:238
  1061.2 69.0 %reduce-scatter.6.cloned.1.call-done = bf16[256,512]{1,0:T(8,128)(2,1)} async-done(((bf16[2048,512]{1,0:T(8,128)(2,1)}), bf16[256,512]{1,0:T(8,128)(2,1)}) %reduce-scatter.6.cloned.1.call-update) | async-done | bytes 262160 | tf_op jit(solution)/shard_map/reduce_scatter | solution.py:232
  1142.0 35.5 %all-reduce.1 = (bf16[2048]{0:T(1024)(128)(2,1)S(1)}, bf16[2048]{0:T(1024)(128)(2,1)S(1)}, bf16[512]{0:T(512)(128)(2,1)S(1)}, bf16[128]{0:T(256)(128)(2,1)S(1)},...) all-reduce(bf16[2048]{0:T(1024)(128)(2,1)S(1)} %get-tuple-element.5, ...), channel_id=1, replica_groups=mesh['dp'=8,'tensor'=4] {'dp'}, use_global_device_ids=true, to_apply=%region_72.73 | all-reduce | flops 14976 | bytes 59904 | tf_op jit(solution)/shard_map/psum | solution.py:249
  1182.8 16.1 %add_add_fusion.2 = (f32[1024,2048]{1,0:T(8,128)}, bf16[1024,2048]{1,0:T(8,128)(2,1)}) fusion(f32[1024,2048]{1,0:T(8,128)} %get-tuple-element.564, f32[1024]{0:T(1024)S(1)} %negate_multiply_fusion, f32[1024]{0:T(1024)S(1)} %multiply_multiply_fusion.2, f32[1024]{0:T(1024)S(1)} %copy-done.37, bf16[1024,2048]{1,0:T(8,128)(2,1)} %param.58, ...), kind=kLoop, calls=%fused_computation.292 | loop fusion | flops 33554432 | bytes 41984000 | tf_op jit(solution)/shard_map/add | solution.py:230
  1200.5 148.0 %reduce-scatter.14.cloned.1.call-done = bf16[2048,256]{1,0:T(8,128)(2,1)} async-done(((bf16[2048,2048]{1,0:T(8,128)(2,1)}), bf16[2048,256]{1,0:T(8,128)(2,1)}) %reduce-scatter.14.cloned.1.call-update) | async-done | bytes 1048592 | tf_op jit(solution)/shard_map/reduce_scatter | solution.py:244
  1351.1 149.0 %reduce-scatter.12.cloned.1.call-done = bf16[256,2048]{1,0:T(8,128)(2,1)} async-done(((bf16[2048,2048]{1,0:T(8,128)(2,1)}), bf16[256,2048]{1,0:T(8,128)(2,1)}) %reduce-scatter.12.cloned.1.call-update) | async-done | bytes 1048592 | tf_op jit(solution)/shard_map/reduce_scatter | solution.py:241
  (262 shorter events, 301.8 us)
Async XLA Ops:
  7.2 352.4 %all-reduce.7.cloned.1.call-start = ((), (), s32[]{:S(2)}) async-start(), calls=%async_computation.5 | async-start | bytes 8388608 | tf_op jit(solution)/shard_map/psum | solution.py:141
  18.0 100.0 %collective-permute-start.6 = (bf16[1024,256]{1,0:T(8,128)(2,1)}, bf16[1024,256]{1,0:T(8,128)(2,1)}, u32[]{:S(2)}, u32[]{:S(2)}) collective-permute-start(bf16[1024,256]{1,0:T(8,128)(2,1)} %fusion.260), channel_id=1, source_target_pairs={{0,28},{1,29},{2,30},{3,31}} | collective-permute-start | bytes 1572872 | tf_op jit(solution)/shard_map/ppermute | solution.py:15
  26.6 84.4 %collective-permute-start.5 = (bf16[1024,256]{1,0:T(8,128)(2,1)}, bf16[1024,256]{1,0:T(8,128)(2,1)}, u32[]{:S(2)}, u32[]{:S(2)}) collective-permute-start(bf16[1024,256]{1,0:T(8,128)(2,1)} %fusion.260), channel_id=1, source_target_pairs={{0,24},{4,28},{1,25},{5,29},{2,26},{6,30},{3,27},{7,31}} | collective-permute-start | bytes 1572872 | tf_op jit(solution)/shard_map/ppermute | solution.py:15
  28.7 82.3 %collective-permute-start.4 = (bf16[1024,256]{1,0:T(8,128)(2,1)}, bf16[1024,256]{1,0:T(8,128)(2,1)}, u32[]{:S(2)}, u32[]{:S(2)}) collective-permute-start(bf16[1024,256]{1,0:T(8,128)(2,1)} %fusion.260), channel_id=1, source_target_pairs={{0,20},{4,24},{8,28},{1,21},{5,25},{9,29},{2,22},{6,26},{10,30},{3... | collective-permute-start | bytes 1572872 | tf_op jit(solution)/shard_map/ppermute | solution.py:15
  30.8 40.4 %collective-permute-start.1 = (bf16[1024,256]{1,0:T(8,128)(2,1)}, bf16[1024,256]{1,0:T(8,128)(2,1)}, u32[]{:S(2)}, u32[]{:S(2)}) collective-permute-start(bf16[1024,256]{1,0:T(8,128)(2,1)} %fusion.260), channel_id=1, source_target_pairs={{0,8},{4,12},{8,16},{12,20},{16,24},{20,28},{1,9},{5,13},{9,17},{1... | collective-permute-start | bytes 1572872 | tf_op jit(solution)/shard_map/ppermute | solution.py:15
  32.9 55.5 %collective-permute-start = (bf16[1024,256]{1,0:T(8,128)(2,1)}, bf16[1024,256]{1,0:T(8,128)(2,1)}, u32[]{:S(2)}, u32[]{:S(2)}) collective-permute-start(bf16[1024,256]{1,0:T(8,128)(2,1)} %fusion.260), channel_id=1, source_target_pairs={{0,4},{4,8},{8,12},{12,16},{16,20},{20,24},{24,28},{1,5},{5,9},{9,... | collective-permute-start | bytes 1572872 | tf_op jit(solution)/shard_map/ppermute | solution.py:15
  71.2 39.4 %collective-permute-start.3 = (bf16[1024,256]{1,0:T(8,128)(2,1)}, bf16[1024,256]{1,0:T(8,128)(2,1)}, u32[]{:S(2)}, u32[]{:S(2)}) collective-permute-start(bf16[1024,256]{1,0:T(8,128)(2,1)} %fusion.260), channel_id=1, source_target_pairs={{0,16},{4,20},{8,24},{12,28},{1,17},{5,21},{9,25},{13,29},{2,18},{... | collective-permute-start | bytes 1572872 | tf_op jit(solution)/shard_map/ppermute | solution.py:15
  88.4 22.1 %collective-permute-start.2 = (bf16[1024,256]{1,0:T(8,128)(2,1)}, bf16[1024,256]{1,0:T(8,128)(2,1)}, u32[]{:S(2)}, u32[]{:S(2)}) collective-permute-start(bf16[1024,256]{1,0:T(8,128)(2,1)} %fusion.260), channel_id=1, source_target_pairs={{0,12},{4,16},{8,20},{12,24},{16,28},{1,13},{5,17},{9,21},{13,25},... | collective-permute-start | bytes 1572872 | tf_op jit(solution)/shard_map/ppermute | solution.py:15
  164.8 336.2 %all-reduce.9.cloned.1.call-start = ((), (), s32[]{:S(2)}) async-start(), calls=%async_computation.6 | async-start | bytes 8388608 | tf_op jit(solution)/shard_map/psum | solution.py:160
  164.9 203.7 %copy-start.42 = (f32[2048]{0:T(1024)S(1)}, f32[2048]{0:T(1024)}, u32[]{:S(2)}) copy-start(f32[2048]{0:T(1024)} %param.67) | copy-start | bytes 24580
  415.3 571.7 %all-reduce.11.cloned.1.call-start = ((), (), s32[]{:S(2)}) async-start(), calls=%async_computation.12 | async-start | bytes 17825792 | tf_op jit(solution)/shard_map/psum | solution.py:151
  559.0 46.0 %collective-permute-start.7 = (bf16[1024,256]{0,1:T(8,128)(2,1)}, bf16[1024,256]{0,1:T(8,128)(2,1)}, u32[]{:S(2)}, u32[]{:S(2)}) collective-permute-start(bf16[1024,256]{0,1:T(8,128)(2,1)} %get-tuple-element.410), channel_id=1, source_target_pairs={{4,0},{8,4},{12,8},{16,12},{20,16},{24,20},{28,24},{5,1},{9,5},{13... | collective-permute-start | bytes 1572872 | tf_op jit(solution)/shard_map/ppermute | solution.py:15
  562.8 74.8 %collective-permute-start.8 = (bf16[1024,256]{0,1:T(8,128)(2,1)}, bf16[1024,256]{0,1:T(8,128)(2,1)}, u32[]{:S(2)}, u32[]{:S(2)}) collective-permute-start(bf16[1024,256]{0,1:T(8,128)(2,1)} %get-tuple-element.411), channel_id=1, source_target_pairs={{8,0},{12,4},{16,8},{20,12},{24,16},{28,20},{9,1},{13,5},{17,9},{2... | collective-permute-start | bytes 1572872 | tf_op jit(solution)/shard_map/ppermute | solution.py:15
  566.8 104.2 %collective-permute-start.9 = (bf16[1024,256]{0,1:T(8,128)(2,1)}, bf16[1024,256]{0,1:T(8,128)(2,1)}, u32[]{:S(2)}, u32[]{:S(2)}) collective-permute-start(bf16[1024,256]{0,1:T(8,128)(2,1)} %get-tuple-element.412), channel_id=1, source_target_pairs={{12,0},{16,4},{20,8},{24,12},{28,16},{13,1},{17,5},{21,9},{25,13},... | collective-permute-start | bytes 1572872 | tf_op jit(solution)/shard_map/ppermute | solution.py:15
  574.5 141.8 %collective-permute-start.10 = (bf16[1024,256]{0,1:T(8,128)(2,1)}, bf16[1024,256]{0,1:T(8,128)(2,1)}, u32[]{:S(2)}, u32[]{:S(2)}) collective-permute-start(bf16[1024,256]{0,1:T(8,128)(2,1)} %get-tuple-element.413), channel_id=1, source_target_pairs={{16,0},{20,4},{24,8},{28,12},{17,1},{21,5},{25,9},{29,13},{18,2},{... | collective-permute-start | bytes 1572872 | tf_op jit(solution)/shard_map/ppermute | solution.py:15
  582.0 167.9 %collective-permute-start.11 = (bf16[1024,256]{0,1:T(8,128)(2,1)}, bf16[1024,256]{0,1:T(8,128)(2,1)}, u32[]{:S(2)}, u32[]{:S(2)}) collective-permute-start(bf16[1024,256]{0,1:T(8,128)(2,1)} %get-tuple-element.414), channel_id=1, source_target_pairs={{20,0},{24,4},{28,8},{21,1},{25,5},{29,9},{22,2},{26,6},{30,10},{2... | collective-permute-start | bytes 1572872 | tf_op jit(solution)/shard_map/ppermute | solution.py:15
  605.0 176.6 %collective-permute-start.12 = (bf16[1024,256]{0,1:T(8,128)(2,1)S(1)}, bf16[1024,256]{0,1:T(8,128)(2,1)S(1)}, u32[]{:S(2)}, u32[]{:S(2)}) collective-permute-start(bf16[1024,256]{0,1:T(8,128)(2,1)S(1)} %copy-done.30), channel_id=1, source_target_pairs={{24,0},{28,4},{25,1},{29,5},{26,2},{30,6},{27,3},{31,7}} | collective-permute-start | bytes 1572872 | tf_op jit(solution)/shard_map/ppermute | solution.py:15
  637.5 187.1 %collective-permute-start.13 = (bf16[1024,256]{0,1:T(8,128)(2,1)S(1)}, bf16[1024,256]{0,1:T(8,128)(2,1)S(1)}, u32[]{:S(2)}, u32[]{:S(2)}) collective-permute-start(bf16[1024,256]{0,1:T(8,128)(2,1)S(1)} %copy-done.32), channel_id=1, source_target_pairs={{28,0},{29,1},{30,2},{31,3}} | collective-permute-start | bytes 1572872 | tf_op jit(solution)/shard_map/ppermute | solution.py:15
  828.0 231.5 %reduce-scatter.10.cloned.1.call-start = ((), (), s32[]{:S(2)}) async-start(), calls=%async_computation.9 | async-start | bytes 2359296 | tf_op jit(solution)/shard_map/reduce_scatter | solution.py:238
  836.0 294.3 %reduce-scatter.6.cloned.1.call-start = ((), (), s32[]{:S(2)}) async-start(), calls=%async_computation.7 | async-start | bytes 2359296 | tf_op jit(solution)/shard_map/reduce_scatter | solution.py:232
  842.1 356.7 %reduce-scatter.8.cloned.1.call-start = ((), (), s32[]{:S(2)}) async-start(), calls=%async_computation.8 | async-start | bytes 1179648 | tf_op jit(solution)/shard_map/reduce_scatter | solution.py:235
  991.6 356.8 %reduce-scatter.14.cloned.1.call-start = ((), (), s32[]{:S(2)}) async-start(), calls=%async_computation.11 | async-start | bytes 9437184 | tf_op jit(solution)/shard_map/reduce_scatter | solution.py:244
  1007.9 492.2 %reduce-scatter.12.cloned.1.call-start = ((), (), s32[]{:S(2)}) async-start(), calls=%async_computation.10 | async-start | bytes 9437184 | tf_op jit(solution)/shard_map/reduce_scatter | solution.py:241
  1182.8 320.1 %copy-start.1 = (bf16[512,2048]{1,0:T(8,128)(2,1)S(1)}, bf16[512,2048]{1,0:T(8,128)(2,1)}, u32[]{:S(2)}) copy-start(bf16[512,2048]{1,0:T(8,128)(2,1)} %param.65) | copy-start | bytes 6291460
  (62 other events, 2374.5 us)
Sparse Core Ops, SparseCore 0:
  164.9 194.6 all-reduce.6
  415.4 85.6 all-reduce.8
  828.1 158.8 all-reduce.10
  990.9 68.4 reduce-scatter.9
  1063.4 66.8 reduce-scatter.5
  1133.5 62.3 reduce-scatter.7
  1200.0 148.4 reduce-scatter.13
  1352.1 148.0 reduce-scatter.11
where the time goes:
time: 1520 us; the launch traced here: 1510 us
  waiting for transfers between devices  1050 us (69%)
  matrix products  183 us (12%)
  other arithmetic  105 us (7%)
  loops' own time  51.6 us (3%)
  starting transfers between devices  47 us (3%)
  blocking collectives  35.5 us (2%)
  local copies, waits for them, and re-layouts  26.4 us (2%)
  between operations  15.7 us (1%)
    ppermute x14, waiting for transfers between devices, shifted(): lax.ppermute(value, axis, [(source, source + steps) for source in range(f...  241 us
    psum x1, waiting for transfers between devices, per_device(): lax.psum(attn_part.astype(jnp.bfloat16), 'tensor').astype(jnp.float32)  195 us
    reduce_scatter x1, waiting for transfers between devices, per_device(): lax.psum_scatter(grad_up_part.astype(jnp.bfloat16), 'dp', scatter_dimensi...  149 us
    reduce_scatter x1, waiting for transfers between devices, per_device(): lax.psum_scatter(grad_down_part.astype(jnp.bfloat16), 'dp', scatter_dimen...  148 us
    psum x1, waiting for transfers between devices, per_device(): lax.psum(mlp_part.astype(jnp.bfloat16), 'tensor').astype(jnp.float32)  145 us
    psum x1, waiting for transfers between devices, per_device(): lax.psum(over_cols(d_pre, up_weight).astype(jnp.bfloat16), 'tensor')  69.7 us
    reduce_scatter x1, waiting for transfers between devices, per_device(): lax.psum_scatter(grad_query_part.astype(jnp.bfloat16), 'dp', scatter_dime...  69 us
    dot_general x5, matrix products, over_rows(): lax.dot_general(left, right, (((0,), (0,)), ((), ())), preferred_element_...  50 us
  transfers between devices with their start and end apart: 22, of which 15 were waited for; matrix products, arithmetic and copies ran while one was open for 11% of the time, Pallas kernels for 0%

commit v1 on v0

--- a/solution.py
+++ b/solution.py
@@ -157,9 +157,9 @@
     d_pre = gelu_pull(over_cols(cotangent, down_weight))[0].astype(jnp.bfloat16)
     grad_up_part = over_rows(normed2, d_pre)
     d_up_bias = jnp.sum(d_pre.astype(jnp.float32), axis=0)
-    d_normed2 = lax.psum(over_cols(d_pre, up_weight).astype(jnp.bfloat16), "tensor").astype(
-        jnp.float32
-    )
+    d_normed2 = jnp.sum(
+        lax.all_gather(over_cols(d_pre, up_weight).astype(jnp.bfloat16), "tensor"), axis=0
+    ).astype(jnp.float32)
     d_middle_norm, d_second_gain, d_second_bias = second_pull(d_normed2)
     d_middle = grad_full + d_middle_norm
     d_output_bias = jnp.sum(d_middle, axis=0)

time: 1520 us -> 1300 us (0.86)
  waiting for transfers between devices: 1050 us -> 805 us
    reduce_scatter x1, waiting for transfers between devices: 149 us -> 0.01 us  [per_device(): lax.psum_scatter(grad_up_part.astype(jnp.bfloat16), 'dp', scatter_dimensi...]
    reduce_scatter x1, waiting for transfers between devices: 148 us -> 0.01 us  [per_device(): lax.psum_scatter(grad_down_part.astype(jnp.bfloat16), 'dp', scatter_dimen...]
    all_gather x0 -> x1, waiting for transfers between devices: none -> 73.1 us  [per_device(): lax.all_gather(over_cols(d_pre, up_weight).astype(jnp.bfloat16), 'tensor')]
    psum x1 -> x0, waiting for transfers between devices: 69.7 us -> none  [per_device(): lax.psum(over_cols(d_pre, up_weight).astype(jnp.bfloat16), 'tensor')]
    ppermute x14, waiting for transfers between devices: 241 us -> 291 us  [shifted(): lax.ppermute(value, axis, [(source, source + steps) for source in range(f...]
    psum x1, waiting for transfers between devices: 145 us -> 163 us  [per_device(): lax.psum(mlp_part.astype(jnp.bfloat16), 'tensor').astype(jnp.float32)]
    reduce_scatter x1, waiting for transfers between devices: 29.5 us -> 14.1 us  [per_device(): lax.psum_scatter(grad_out_part.astype(jnp.bfloat16), 'dp', scatter_dimens...]
  transfers between devices with their start and end apart: 22 -> 22, of which waited for: 15 -> 11; matrix products, arithmetic and copies ran while one was open for 11% -> 17% of each run, Pallas kernels for 0% -> 0%
where the time goes in v1:
time: 1300 us; the launch traced here: 1290 us
  waiting for transfers between devices  805 us (62%)
  matrix products  181 us (14%)
  other arithmetic  116 us (9%)
  loops' own time  62.6 us (5%)
  starting transfers between devices  47.3 us (4%)
  blocking collectives  37.2 us (3%)
  local copies, waits for them, and re-layouts  29.2 us (2%)
  between operations  15.9 us (1%)
    ppermute x14, waiting for transfers between devices, shifted(): lax.ppermute(value, axis, [(source, source + steps) for source in range(f...  291 us
    psum x1, waiting for transfers between devices, per_device(): lax.psum(attn_part.astype(jnp.bfloat16), 'tensor').astype(jnp.float32)  195 us
    psum x1, waiting for transfers between devices, per_device(): lax.psum(mlp_part.astype(jnp.bfloat16), 'tensor').astype(jnp.float32)  163 us
    all_gather x1, waiting for transfers between devices, per_device(): lax.all_gather(over_cols(d_pre, up_weight).astype(jnp.bfloat16), 'tensor')  73.1 us
    reduce_scatter x1, waiting for transfers between devices, per_device(): lax.psum_scatter(grad_query_part.astype(jnp.bfloat16), 'dp', scatter_dime...  68.7 us
    dot_general x5, matrix products, over_cols(): lax.dot_general(left, right, (((1,), (1,)), ((), ())), preferred_element_...  50 us
    dot_general x5, matrix products, over_rows(): lax.dot_general(left, right, (((0,), (0,)), ((), ())), preferred_element_...  47.8 us
    ppermute x14, starting transfers between devices, shifted(): lax.ppermute(value, axis, [(source, source + steps) for source in range(f...  46.7 us
  transfers between devices with their start and end apart: 22, of which 11 were waited for; matrix products, arithmetic and copies ran while one was open for 17% of the time, Pallas kernels for 0%

profile of v1, /device:TPU:0, one launch (start us, length us, event | category | flops | bytes accessed | tf_op | source)
XLA Modules:
  0.0 1294.3 jit_solution(15611448168553172606)
XLA Ops:
  46.6 24.5 %collective-permute-done.1 = bf16[1024,256]{1,0:T(8,128)(2,1)} collective-permute-done((bf16[1024,256]{1,0:T(8,128)(2,1)}, bf16[1024,256]{1,0:T(8,128)(2,1)}, u32[]{:S(2)}, u32[]{:S(2)}) %collective-permute-start.1) | collective-permute-done | bytes 524320 | tf_op jit(solution)/shard_map/ppermute | solution.py:15
  71.2 17.3 %collective-permute-start.3 = (bf16[1024,256]{1,0:T(8,128)(2,1)}, bf16[1024,256]{1,0:T(8,128)(2,1)}, u32[]{:S(2)}, u32[]{:S(2)}) collective-permute-start(bf16[1024,256]{1,0:T(8,128)(2,1)} %fusion.260), channel_id=1, source_target_pairs={{0,16},{4,20},{8,24},{12,28},{1,17},{5,21},{9,25},{13,29},{2,18},{... | collective-permute-start | bytes 1572872 | tf_op jit(solution)/shard_map/ppermute | solution.py:15
  100.1 10.5 collective-permute-done.2
  124.7 11.5 convolution_bitcast_fusion.14
  146.7 9.8 conditional.33
  162.9 194.6 %all-reduce.6.cloned.1.call-done = bf16[1024,2048]{1,0:T(8,128)(2,1)} async-done(((bf16[1024,2048]{1,0:T(8,128)(2,1)}), bf16[1024,2048]{1,0:T(8,128)(2,1)}) %all-reduce.6.cloned.1.call-update) | async-done | bytes 4194320 | tf_op jit(solution)/shard_map/psum | solution.py:141
  366.4 13.9 %fusion.277 = f32[1024,2048]{1,0:T(8,128)} fusion(bf16[2048,2048]{1,0:T(8,128)(2,1)} %param.69, f32[2048]{0:T(1024)S(1)} %copy-done.78, f32[2048]{0:T(1024)S(1)} %copy-done.63, f32[1024]{0:T(1024)S(1)} %fusion.273, bf16[1024,2048]{1,0:T(8,128)(2,1)S(1)} %copy-done.23, bf16[1024,2048]{1,0:T(8,128)(2,1)S(1)} %copy-done.3, ...), kind=kOutput, calls=%fused_computation.360 | convolution fusion | flops 8608808960 | bytes 25198592 | tf_op jit(solution)/shard_map/dot_general | solution.py:146
  380.3 20.6 %fusion.282 = (bf16[2048]{0:T(1024)(128)(2,1)}, bf16[1024,2048]{1,0:T(8,128)(2,1)}) fusion(f32[1024,2048]{1,0:T(8,128)} %fusion.277, f32[2048]{0:T(1024)S(1)} %copy-done.79, bf16[1024,2048]{1,0:T(8,128)(2,1)S(1)} %copy-done.30, bf16[2048,2048]{1,0:T(8,128)(2,1)} %param.71), kind=kOutput, calls=%fused_computation.363 | convolution fusion | flops 8636069888 | bytes 25178112 | tf_op jit(solution)/shard_map/dot_general | solution.py:36
  400.9 12.2 convolution_convert_fusion.3
  413.2 16.7 %convolution_convert_fusion = bf16[2048,2048]{1,0:T(8,128)(2,1)} fusion(bf16[1024,2048]{1,0:T(8,128)(2,1)} %param.73, f32[1024,2048]{1,0:T(8,128)} %fusion.277, f32[2048]{0:T(1024)S(1)} %copy-done.79), kind=kOutput, calls=%fused_computation.299 | convolution fusion | flops 8615100416 | bytes 20979712 | tf_op jit(solution)/shard_map/dot_general | solution.py:30
  429.9 16.3 %convolution_convert_fusion.1 = bf16[2048,2048]{1,0:T(8,128)(2,1)} fusion(bf16[1024,2048]{1,0:T(8,128)(2,1)} %get-tuple-element.562, f32[2048]{0:T(1024)S(1)} %copy-done.78, f32[2048]{0:T(1024)S(1)} %copy-done.63, f32[1024]{0:T(1024)S(1)} %fusion.273, bf16[1024,2048]{1,0:T(8,128)(2,1)} %all-reduce.6.cloned.1.call-done, bf16[1024,2048]{1,0:T(8,128)(2,1)} %param.58, ...), kind=kOutput, calls=%fused_computation.300 | convolution fusion | flops 8613003264 | bytes 21004288 | tf_op jit(solution)/shard_map/dot_general | solution.py:30
  446.3 73.1 %all-gather.3.cloned.1.call-done = bf16[4096,2048]{1,0:T(8,128)(2,1)} async-done(((bf16[1024,2048]{1,0:T(8,128)(2,1)}), bf16[4096,2048]{1,0:T(8,128)(2,1)}) %all-gather.3.cloned.1.call-update) | async-done | bytes 16777232 | tf_op jit(solution)/shard_map/all_gather | solution.py:161
  519.3 12.5 reduce_sum.291
  601.5 14.6 %conditional.41 = (bf16[1024,256]{0,1:T(8,128)(2,1)}, f32[1024,4,128]{0,2,1:T(8,128)}) conditional(s32[]{:T(128)} %convert_element_type.309, () %tuple.196, (bf16[1024,256]{1,0:T(8,128)(2,1)}, bf16[1024,4,128]{0,2,1:T(8,128)(2,1)S(1)}, f32[4,1024]{1,0:T(4,128)S(1)}, bf16[1024,4,128]{0,2,1:T(8,128)(2,1)}, f32[4,1024]{1,0:T(4,128)S(1)}) %tuple.370), branch_computations={%region_65.66_spmd, %region_66.67_spmd} | conditional | flops 5394923520 | bytes 159694928 | solution.py:210
  644.0 16.2 %convolution_convert_fusion.4 = bf16[1024,2048]{1,0:T(8,128)(2,1)} fusion(bf16[2048,2048]{1,0:T(8,128)(2,1)} %param.71, f32[1024,2048]{1,0:T(8,128)} %fusion.277, f32[2048]{0:T(1024)S(1)} %copy-done.80), kind=kOutput, calls=%fused_computation.306 | convolution fusion | flops 8613003264 | bytes 20979712 | tf_op jit(solution)/shard_map/dot_general | solution.py:149
  676.3 30.7 %collective-permute-done.7 = bf16[1024,256]{0,1:T(8,128)(2,1)S(1)} collective-permute-done((bf16[1024,256]{0,1:T(8,128)(2,1)S(1)}, bf16[1024,256]{0,1:T(8,128)(2,1)S(1)}, u32[]{:S(2)}, u32[]{:S(2)}) %collective-permute-start.7) | collective-permute-done | bytes 524320 | tf_op jit(solution)/shard_map/ppermute | solution.py:15
  708.3 66.2 %collective-permute-done.8 = bf16[1024,256]{0,1:T(8,128)(2,1)S(1)} collective-permute-done((bf16[1024,256]{0,1:T(8,128)(2,1)S(1)}, bf16[1024,256]{0,1:T(8,128)(2,1)S(1)}, u32[]{:S(2)}, u32[]{:S(2)}) %collective-permute-start.8) | collective-permute-done | bytes 524320 | tf_op jit(solution)/shard_map/ppermute | solution.py:15
  783.2 56.8 %collective-permute-done.10 = bf16[1024,256]{0,1:T(8,128)(2,1)S(1)} collective-permute-done((bf16[1024,256]{0,1:T(8,128)(2,1)S(1)}, bf16[1024,256]{0,1:T(8,128)(2,1)S(1)}, u32[]{:S(2)}, u32[]{:S(2)}) %collective-permute-start.10) | collective-permute-done | bytes 524320 | tf_op jit(solution)/shard_map/ppermute | solution.py:15
  840.0 102.5 %collective-permute-done.11 = bf16[1024,256]{0,1:T(8,128)(2,1)S(1)} collective-permute-done((bf16[1024,256]{0,1:T(8,128)(2,1)S(1)}, bf16[1024,256]{0,1:T(8,128)(2,1)S(1)}, u32[]{:S(2)}, u32[]{:S(2)}) %collective-permute-start.11) | collective-permute-done | bytes 524320 | tf_op jit(solution)/shard_map/ppermute | solution.py:15
  962.6 14.1 %reduce-scatter.10.cloned.1.call-done = bf16[512,256]{1,0:T(8,128)(2,1)} async-done(((bf16[512,2048]{1,0:T(8,128)(2,1)}), bf16[512,256]{1,0:T(8,128)(2,1)}) %reduce-scatter.10.cloned.1.call-update) | async-done | bytes 262160 | tf_op jit(solution)/shard_map/reduce_scatter | solution.py:238
  978.5 68.7 %reduce-scatter.6.cloned.1.call-done = bf16[256,512]{1,0:T(8,128)(2,1)} async-done(((bf16[2048,512]{1,0:T(8,128)(2,1)}), bf16[256,512]{1,0:T(8,128)(2,1)}) %reduce-scatter.6.cloned.1.call-update) | async-done | bytes 262160 | tf_op jit(solution)/shard_map/reduce_scatter | solution.py:232
  1049.0 163.0 %all-reduce.8.cloned.1.call-done = (bf16[1024,2048]{1,0:T(8,128)(2,1)}, bf16[1024,2048]{1,0:T(8,128)(2,1)}, bf16[1024,256]{0,1:T(8,128)(2,1)}) async-done(((bf16[1024,2048]{1,0:T(8,128)(2,1)}, bf16[1024,2048]{1,0:T(8,128)(2,1)}, bf16[1024,256]{0,1:T(8,128)(2,1)}), (bf16[1024,2048]{1,0:T(8,128)(2,1)}, bf16[1024,2048]{1,0:T(8,128)(2,1)}, bf16[1024,256]{0,1:T(8,128)(2,1)})) %all-reduce.8.cloned.1.call-update) | async-done | bytes 8912912 | tf_op jit(solution)/shard_map/psum | solution.py:151
  1226.8 37.2 %all-reduce.1 = (bf16[2048]{0:T(1024)(128)(2,1)S(1)}, bf16[2048]{0:T(1024)(128)(2,1)S(1)}, bf16[512]{0:T(512)(128)(2,1)S(1)}, bf16[128]{0:T(256)(128)(2,1)S(1)},...) all-reduce(bf16[2048]{0:T(1024)(128)(2,1)S(1)} %get-tuple-element.5, ...), channel_id=1, replica_groups=mesh['dp'=8,'tensor'=4] {'dp'}, use_global_device_ids=true, to_apply=%region_72.73 | all-reduce | flops 14976 | bytes 59904 | tf_op jit(solution)/shard_map/psum | solution.py:249
  1269.3 16.1 %add_add_fusion.2 = (f32[1024,2048]{1,0:T(8,128)}, bf16[1024,2048]{1,0:T(8,128)(2,1)}) fusion(f32[1024,2048]{1,0:T(8,128)} %copy-done.27, f32[1024]{0:T(1024)S(1)} %negate_multiply_fusion, f32[1024]{0:T(1024)S(1)} %multiply_multiply_fusion.2, f32[1024]{0:T(1024)S(1)} %copy-done.60, bf16[1024,2048]{1,0:T(8,128)(2,1)} %param.58, f32[1024]{0:T(1024)S(1)} %copy-done.65, ...), kind=kLoop, calls=%fused_computation.292 | loop fusion | flops 33554432 | bytes 41984000 | tf_op jit(solution)/shard_map/add | solution.py:230
  (279 shorter events, 269.9 us)
Async XLA Ops:
  7.2 350.3 %all-reduce.6.cloned.1.call-start = ((), (), s32[]{:S(2)}) async-start(), calls=%async_computation.5 | async-start | bytes 8388608 | tf_op jit(solution)/shard_map/psum | solution.py:141
  18.0 100.0 %collective-permute-start.6 = (bf16[1024,256]{1,0:T(8,128)(2,1)}, bf16[1024,256]{1,0:T(8,128)(2,1)}, u32[]{:S(2)}, u32[]{:S(2)}) collective-permute-start(bf16[1024,256]{1,0:T(8,128)(2,1)} %fusion.260), channel_id=1, source_target_pairs={{0,28},{1,29},{2,30},{3,31}} | collective-permute-start | bytes 1572872 | tf_op jit(solution)/shard_map/ppermute | solution.py:15
  26.6 84.4 %collective-permute-start.5 = (bf16[1024,256]{1,0:T(8,128)(2,1)}, bf16[1024,256]{1,0:T(8,128)(2,1)}, u32[]{:S(2)}, u32[]{:S(2)}) collective-permute-start(bf16[1024,256]{1,0:T(8,128)(2,1)} %fusion.260), channel_id=1, source_target_pairs={{0,24},{4,28},{1,25},{5,29},{2,26},{6,30},{3,27},{7,31}} | collective-permute-start | bytes 1572872 | tf_op jit(solution)/shard_map/ppermute | solution.py:15
  28.7 82.3 %collective-permute-start.4 = (bf16[1024,256]{1,0:T(8,128)(2,1)}, bf16[1024,256]{1,0:T(8,128)(2,1)}, u32[]{:S(2)}, u32[]{:S(2)}) collective-permute-start(bf16[1024,256]{1,0:T(8,128)(2,1)} %fusion.260), channel_id=1, source_target_pairs={{0,20},{4,24},{8,28},{1,21},{5,25},{9,29},{2,22},{6,26},{10,30},{3... | collective-permute-start | bytes 1572872 | tf_op jit(solution)/shard_map/ppermute | solution.py:15
  30.8 40.3 %collective-permute-start.1 = (bf16[1024,256]{1,0:T(8,128)(2,1)}, bf16[1024,256]{1,0:T(8,128)(2,1)}, u32[]{:S(2)}, u32[]{:S(2)}) collective-permute-start(bf16[1024,256]{1,0:T(8,128)(2,1)} %fusion.260), channel_id=1, source_target_pairs={{0,8},{4,12},{8,16},{12,20},{16,24},{20,28},{1,9},{5,13},{9,17},{1... | collective-permute-start | bytes 1572872 | tf_op jit(solution)/shard_map/ppermute | solution.py:15
  32.9 55.5 %collective-permute-start = (bf16[1024,256]{1,0:T(8,128)(2,1)}, bf16[1024,256]{1,0:T(8,128)(2,1)}, u32[]{:S(2)}, u32[]{:S(2)}) collective-permute-start(bf16[1024,256]{1,0:T(8,128)(2,1)} %fusion.260), channel_id=1, source_target_pairs={{0,4},{4,8},{8,12},{12,16},{16,20},{20,24},{24,28},{1,5},{5,9},{9,... | collective-permute-start | bytes 1572872 | tf_op jit(solution)/shard_map/ppermute | solution.py:15
  71.2 39.4 %collective-permute-start.3 = (bf16[1024,256]{1,0:T(8,128)(2,1)}, bf16[1024,256]{1,0:T(8,128)(2,1)}, u32[]{:S(2)}, u32[]{:S(2)}) collective-permute-start(bf16[1024,256]{1,0:T(8,128)(2,1)} %fusion.260), channel_id=1, source_target_pairs={{0,16},{4,20},{8,24},{12,28},{1,17},{5,21},{9,25},{13,29},{2,18},{... | collective-permute-start | bytes 1572872 | tf_op jit(solution)/shard_map/ppermute | solution.py:15
  88.5 22.1 %collective-permute-start.2 = (bf16[1024,256]{1,0:T(8,128)(2,1)}, bf16[1024,256]{1,0:T(8,128)(2,1)}, u32[]{:S(2)}, u32[]{:S(2)}) collective-permute-start(bf16[1024,256]{1,0:T(8,128)(2,1)} %fusion.260), channel_id=1, source_target_pairs={{0,12},{4,16},{8,20},{12,24},{16,28},{1,13},{5,17},{9,21},{13,25},... | collective-permute-start | bytes 1572872 | tf_op jit(solution)/shard_map/ppermute | solution.py:15
  162.9 356.5 %all-gather.3.cloned.1.call-start = ((), (), s32[]{:S(2)}) async-start(), calls=%async_computation.11 | async-start | bytes 20971520 | tf_op jit(solution)/shard_map/all_gather | solution.py:161
  413.1 534.2 %reduce-scatter.14.cloned.1.call-start = ((), (), s32[]{:S(2)}) async-start(), calls=%async_computation.10 | async-start | bytes 9437184 | tf_op jit(solution)/shard_map/reduce_scatter | solution.py:244
  429.9 520.1 %reduce-scatter.12.cloned.1.call-start = ((), (), s32[]{:S(2)}) async-start(), calls=%async_computation.9 | async-start | bytes 9437184 | tf_op jit(solution)/shard_map/reduce_scatter | solution.py:241
  446.2 530.5 %reduce-scatter.10.cloned.1.call-start = ((), (), s32[]{:S(2)}) async-start(), calls=%async_computation.8 | async-start | bytes 2359296 | tf_op jit(solution)/shard_map/reduce_scatter | solution.py:238
  559.1 488.1 %reduce-scatter.6.cloned.1.call-start = ((), (), s32[]{:S(2)}) async-start(), calls=%async_computation.6 | async-start | bytes 2359296 | tf_op jit(solution)/shard_map/reduce_scatter | solution.py:232
  643.9 568.2 %all-reduce.8.cloned.1.call-start = ((), (), s32[]{:S(2)}) async-start(), calls=%async_computation.12 | async-start | bytes 17825792 | tf_op jit(solution)/shard_map/psum | solution.py:151
  660.2 46.8 %collective-permute-start.7 = (bf16[1024,256]{0,1:T(8,128)(2,1)S(1)}, bf16[1024,256]{0,1:T(8,128)(2,1)S(1)}, u32[]{:S(2)}, u32[]{:S(2)}) collective-permute-start(bf16[1024,256]{0,1:T(8,128)(2,1)S(1)} %copy-done.45), channel_id=1, source_target_pairs={{4,0},{8,4},{12,8},{16,12},{20,16},{24,20},{28,24},{5,1},{9,5},{13... | collective-permute-start | bytes 1572872 | tf_op jit(solution)/shard_map/ppermute | solution.py:15
  661.6 112.9 %collective-permute-start.8 = (bf16[1024,256]{0,1:T(8,128)(2,1)S(1)}, bf16[1024,256]{0,1:T(8,128)(2,1)S(1)}, u32[]{:S(2)}, u32[]{:S(2)}) collective-permute-start(bf16[1024,256]{0,1:T(8,128)(2,1)S(1)} %copy-done.47), channel_id=1, source_target_pairs={{8,0},{12,4},{16,8},{20,12},{24,16},{28,20},{9,1},{13,5},{17,9},{2... | collective-permute-start | bytes 1572872 | tf_op jit(solution)/shard_map/ppermute | solution.py:15
  672.1 111.0 %collective-permute-start.9 = (bf16[1024,256]{0,1:T(8,128)(2,1)S(1)}, bf16[1024,256]{0,1:T(8,128)(2,1)S(1)}, u32[]{:S(2)}, u32[]{:S(2)}) collective-permute-start(bf16[1024,256]{0,1:T(8,128)(2,1)S(1)} %copy-done.49), channel_id=1, source_target_pairs={{12,0},{16,4},{20,8},{24,12},{28,16},{13,1},{17,5},{21,9},{25,13},... | collective-permute-start | bytes 1572872 | tf_op jit(solution)/shard_map/ppermute | solution.py:15
  673.7 166.3 %collective-permute-start.10 = (bf16[1024,256]{0,1:T(8,128)(2,1)S(1)}, bf16[1024,256]{0,1:T(8,128)(2,1)S(1)}, u32[]{:S(2)}, u32[]{:S(2)}) collective-permute-start(bf16[1024,256]{0,1:T(8,128)(2,1)S(1)} %copy-done.51), channel_id=1, source_target_pairs={{16,0},{20,4},{24,8},{28,12},{17,1},{21,5},{25,9},{29,13},{18,2},{... | collective-permute-start | bytes 1572872 | tf_op jit(solution)/shard_map/ppermute | solution.py:15
  675.0 267.5 %collective-permute-start.11 = (bf16[1024,256]{0,1:T(8,128)(2,1)S(1)}, bf16[1024,256]{0,1:T(8,128)(2,1)S(1)}, u32[]{:S(2)}, u32[]{:S(2)}) collective-permute-start(bf16[1024,256]{0,1:T(8,128)(2,1)S(1)} %copy-done.53), channel_id=1, source_target_pairs={{20,0},{24,4},{28,8},{21,1},{25,5},{29,9},{22,2},{26,6},{30,10},{2... | collective-permute-start | bytes 1572872 | tf_op jit(solution)/shard_map/ppermute | solution.py:15
  707.0 235.5 %collective-permute-start.12 = (bf16[1024,256]{0,1:T(8,128)(2,1)S(1)}, bf16[1024,256]{0,1:T(8,128)(2,1)S(1)}, u32[]{:S(2)}, u32[]{:S(2)}) collective-permute-start(bf16[1024,256]{0,1:T(8,128)(2,1)S(1)} %copy-done.55), channel_id=1, source_target_pairs={{24,0},{28,4},{25,1},{29,5},{26,2},{30,6},{27,3},{31,7}} | collective-permute-start | bytes 1572872 | tf_op jit(solution)/shard_map/ppermute | solution.py:15
  774.4 168.1 %collective-permute-start.13 = (bf16[1024,256]{0,1:T(8,128)(2,1)}, bf16[1024,256]{0,1:T(8,128)(2,1)S(1)}, u32[]{:S(2)}, u32[]{:S(2)}) collective-permute-start(bf16[1024,256]{0,1:T(8,128)(2,1)} %get-tuple-element.416), channel_id=1, source_target_pairs={{28,0},{29,1},{30,2},{31,3}} | collective-permute-start | bytes 1572872 | tf_op jit(solution)/shard_map/ppermute | solution.py:15
  944.1 341.2 %reduce-scatter.8.cloned.1.call-start = ((), (), s32[]{:S(2)}) async-start(), calls=%async_computation.7 | async-start | bytes 1179648 | tf_op jit(solution)/shard_map/reduce_scatter | solution.py:235
  962.5 254.3 %copy-start.60 = (f32[1024]{0:T(1024)S(1)}, f32[1024]{0:T(1024)}, u32[]{:S(2)}) copy-start(f32[1024]{0:T(1024)} %copy-done.59) | copy-start | bytes 12292
  962.5 254.3 %copy-start.62 = (f32[2048]{0:T(1024)S(1)}, f32[2048]{0:T(1024)}, u32[]{:S(2)}) copy-start(f32[2048]{0:T(1024)} %param.59) | copy-start | bytes 24580
  (70 other events, 2260.2 us)
Sparse Core Ops, SparseCore 0:
  163.0 194.5 all-reduce.5
  413.2 106.0 all-gather.2
  523.4 149.3 reduce-scatter.13
  676.3 175.0 reduce-scatter.11
  855.2 121.4 reduce-scatter.9
  980.5 66.6 reduce-scatter.5
  1050.9 161.1 all-reduce.7
  1216.9 63.4 reduce-scatter.7
